TPU v7x, 512 devices: a whole 4x8x8 slice. The times are simulated.
512 devices in a mesh: row: 32 (over y_hi, z, core), col: 16 (over x, y_lo).
Axes of the slice: x: 4, y: 8 (y_hi: 2, y_lo: 4; y = y_hi * 4 + y_lo), z: 8, core: 2. Of those that a mesh axis runs over, the one named last changes fastest.
Arguments:
- curve_embed: bfloat16 [32768, 128], P(('row', 'col')), may hold values from -6 to 6
- solution: float32 [32768, 256], P(('row', 'col')), may hold values from -0.125 to 0.125
- targets: bfloat16 [32768, 256], P(('row', 'col')), may hold values from -6 to 6
- lengths: int32 [32768], P(('row', 'col')), may hold values from 1 to 256
- slot_curve: int32 [32768], P(('row', 'col')), may hold values from 0 to 32767, as said below
- epoch_kernel: float32 [256, 256], replicated, as said below
Outputs:
- row_grad: float32 [32768, 128], P(('row', 'col'))
- col_grad: float32 [32768, 128], P(('row', 'col'))
Inputs may be any that keep to these rules, and one draw needn't show every extreme that they name: Within each aligned group of 1024 slots, slot_curve is a permutation of that group's own slot numbers. `epoch_kernel`: symmetric positive definite.
All inputs are finite; a program needn't handle non-finite values.
Results may differ from a plain program's by a relative error of at most 0.0036.
Values may be sent and summed in bfloat16 or wider, within the bound.
A program may use at most 64 MiB of HBM per device.

v0:
```python
import jax
import jax.numpy as jnp
from jax import lax
from jax.sharding import Mesh
from jax.sharding import PartitionSpec as P

ROW = ("row_0", "row_1", "row_2")
ROW_COL = ("row_0", "row_1", "row_2", "col")


def sent_to_all(x, axis):
    copies = jnp.broadcast_to(x, (lax.axis_size(axis), *x.shape))
    return lax.all_to_all(copies, axis, split_axis=0, concat_axis=0, tiled=True)


def in_order(blocks, dim):
    blocks = jnp.moveaxis(blocks, 0, dim)
    lengths = blocks.shape
    return blocks.reshape(*lengths[:dim], lengths[dim] * lengths[dim + 1], *lengths[dim + 2 :])


def collect(x, axis, dim):
    blocks = sent_to_all(x, axis)
    return in_order(blocks, dim)


def whole_of(x, axes, dim):
    far, near = axes
    blocks = sent_to_all(sent_to_all(x, far), near)
    return in_order(blocks.swapaxes(0, 1).reshape(-1, *x.shape), dim)


def in_one_piece(arrays, axis, dim, along):
    both = jnp.concatenate(arrays, axis=along)
    result, at, gathered = (whole_of(both, axis, dim), 0, [])
    for a in arrays:
        gathered.append(lax.slice_in_dim(result, at, at + a.shape[along], axis=along))
        at += a.shape[along]
    return tuple(gathered)


def cut_along(x, dim, size):
    lengths = x.shape
    blocks = x.reshape(*lengths[:dim], size, lengths[dim] // size, *lengths[dim + 1 :])
    return jnp.moveaxis(blocks, dim, 0)


def summed_on_arrival(x, axis, dim):
    blocks = cut_along(x, dim, lax.axis_size(axis))
    arrived = lax.all_to_all(blocks, axis, split_axis=0, concat_axis=0, tiled=True)
    return arrived.astype(jnp.float32).sum(axis=0)


def kernel_block(row_embed, row_square, piece_embed):
    piece_wide = piece_embed.astype(jnp.float32)
    products = lax.dot_general(
        row_embed, piece_embed, (((1,), (1,)), ((), ())), preferred_element_type=jnp.float32
    )
    distance = (
        row_square[:, None] + jnp.sum(piece_wide * piece_wide, axis=1)[None, :] - 2.0 * products
    )
    return jnp.exp(-distance / row_embed.shape[1])


def block_width():
    return 256


def make_fit(row_embed, row_square):

    def fit_fold(summed, pieces, offset):
        piece_embed, piece_fitted = pieces
        extent = piece_embed.shape[0]
        width_blk = block_width()

        def fit_advance(position, running):
            embed_part = lax.dynamic_slice_in_dim(piece_embed, position * width_blk, width_blk, 0)
            fitted_part = lax.dynamic_slice_in_dim(piece_fitted, position * width_blk, width_blk, 0)
            kernel = kernel_block(row_embed, row_square, embed_part).astype(jnp.bfloat16)
            return running + jnp.dot(kernel, fitted_part, preferred_element_type=jnp.float32)

        return lax.fori_loop(0, extent // width_blk, fit_advance, summed)

    return fit_fold


def make_grad(row_embed, row_square, row_wide, adjoint):

    def grad_fold(carry, pieces, offset):
        piece_embed, piece_fitted = pieces
        extent = piece_embed.shape[0]
        width_blk = block_width()

        def grad_advance(position, running):
            row_part, col_part = running
            embed_part = lax.dynamic_slice_in_dim(piece_embed, position * width_blk, width_blk, 0)
            fitted_part = lax.dynamic_slice_in_dim(piece_fitted, position * width_blk, width_blk, 0)
            kernel = kernel_block(row_embed, row_square, embed_part)
            link = lax.dot_general(
                adjoint, fitted_part, (((1,), (1,)), ((), ())), preferred_element_type=jnp.float32
            )
            weight = (link * kernel).astype(jnp.bfloat16)
            across = (
                jnp.dot(weight, embed_part, preferred_element_type=jnp.float32)
                - row_wide * jnp.sum(weight, axis=1, dtype=jnp.float32)[:, None]
            )
            down = lax.dot_general(
                weight, row_embed, (((0,), (0,)), ((), ())), preferred_element_type=jnp.float32
            )
            down = (
                down
                - embed_part.astype(jnp.float32)
                * jnp.sum(weight, axis=0, dtype=jnp.float32)[:, None]
            )
            first_row = offset + position * width_blk
            col_part = lax.dynamic_update_slice_in_dim(col_part, down, first_row, 0)
            return (row_part + across, col_part)

        return lax.fori_loop(0, extent // width_blk, grad_advance, carry)

    return grad_fold


def per_device(curve_embed, solution, targets, lengths, slot_curve, epoch_kernel):
    own_rows = curve_embed.shape[0]
    width = curve_embed.shape[1]
    epochs_count = solution.shape[1]
    group_size = own_rows * lax.axis_size("col")
    column_size = own_rows * lax.axis_size(ROW)
    fitted_own = jnp.dot(
        solution, epoch_kernel, precision=lax.Precision.HIGHEST, preferred_element_type=jnp.float32
    ).astype(jnp.bfloat16)
    row_embed, row_curve = (collect(curve_embed, "col", 0), collect(slot_curve, "col", 0))
    row_wide = row_embed.astype(jnp.float32)
    row_square = jnp.sum(row_wide * row_wide, axis=1)
    fit_fold = make_fit(row_embed, row_square)
    start_fit = jnp.zeros((group_size, epochs_count), jnp.float32)
    col_embed, col_fitted = in_one_piece(
        (curve_embed, fitted_own), (("row_0", "row_1"), "row_2"), 0, 1
    )
    fitted_sum = fit_fold(start_fit, (col_embed, col_fitted), 0)
    epochs = jnp.arange(epochs_count, dtype=jnp.int32)
    fitted_mine = summed_on_arrival(fitted_sum.astype(jnp.bfloat16), "col", 0)
    observed = epochs[None, :] < lengths[:, None]
    adjoint_own = jnp.where(observed, targets.astype(jnp.float32) - fitted_mine, 0.0).astype(
        jnp.bfloat16
    )
    adjoint = collect(adjoint_own, "col", 0)
    grad_fold = make_grad(row_embed, row_square, row_wide, adjoint)
    start_grad = (
        jnp.zeros((group_size, width), jnp.float32),
        jnp.zeros((column_size, width), jnp.float32),
    )
    row_sum, col_sum = grad_fold(start_grad, (col_embed, col_fitted), 0)
    group_base = lax.axis_index(ROW) * group_size
    local_curve = (row_curve - group_base).astype(jnp.int32)
    inverse = (
        jnp.zeros((group_size,), jnp.int32)
        .at[local_curve]
        .set(jnp.arange(group_size, dtype=jnp.int32))
    )
    reordered = jnp.take(row_sum, inverse, axis=0)
    factor = 2.0 / width
    row_grad = summed_on_arrival(reordered.astype(jnp.bfloat16), "col", 0) * factor
    col_grad = summed_on_arrival(col_sum.astype(jnp.bfloat16), ROW, 0) * factor
    return (row_grad, col_grad)


def solution(mesh):
    split = Mesh(
        mesh.devices.reshape(2, 8, 2, mesh.shape["col"]), ("row_0", "row_1", "row_2", "col")
    )
    return jax.shard_map(
        per_device,
        mesh=split,
        in_specs=(
            P(ROW_COL, None),
            P(ROW_COL, None),
            P(ROW_COL, None),
            P(ROW_COL),
            P(ROW_COL),
            P(),
        ),
        out_specs=(P(ROW_COL, None), P(ROW_COL, None)),
        check_vma=False,
    )
```

profile of v0, /device:TPU:1, one launch (start us, length us, event | category | flops | bytes accessed | tf_op | source)
XLA Modules:
  0.0 196.1 jit_solution(16008316509491605748)
XLA Ops:
  0.6 1.5 broadcast_in_dim.71
  2.1 8.0 %all-to-all-start.3 = ((bf16[16,64,128]{2,1,0:T(8,128)(2,1)}), bf16[16,64,128]{2,1,0:T(8,128)(2,1)S(1)}, u32[]{:S(2)}, u32[]{:S(2)}) async-start(bf16[16,64,128]{2,1,0:T(8,128)(2,1)} %broadcast_in_dim.71), calls=%async_computation.3 | async-start | bytes 524288 | tf_op jit(solution)/shard_map/all_to_all | solution.py:13
  12.0 6.2 %all-to-all-done.3 = bf16[16,64,128]{2,1,0:T(8,128)(2,1)S(1)} async-done(((bf16[16,64,128]{2,1,0:T(8,128)(2,1)}), bf16[16,64,128]{2,1,0:T(8,128)(2,1)S(1)}, u32[]{:S(2)}, u32[]{:S(2)}) %all-to-all-start.3) | async-done | bytes 262176 | tf_op jit(solution)/shard_map/all_to_all | solution.py:13
  19.1 14.6 %all-to-all-start.1 = ((bf16[16,64,384]{2,1,0:T(8,128)(2,1)}), bf16[16,64,384]{2,1,0:T(8,128)(2,1)S(1)}, u32[]{:S(2)}, u32[]{:S(2)}) async-start(bf16[16,64,384]{2,1,0:T(8,128)(2,1)} %broadcast_in_dim.68), calls=%async_computation.1 | async-start | bytes 1572864 | tf_op jit(solution)/shard_map/all_to_all | solution.py:13
  34.0 17.8 %all-to-all-done.1 = bf16[16,64,384]{2,1,0:T(8,128)(2,1)S(1)} async-done(((bf16[16,64,384]{2,1,0:T(8,128)(2,1)}), bf16[16,64,384]{2,1,0:T(8,128)(2,1)S(1)}, u32[]{:S(2)}, u32[]{:S(2)}) %all-to-all-start.1) | async-done | bytes 786464 | tf_op jit(solution)/shard_map/all_to_all | solution.py:13
  52.1 8.7 %all_to_all.41 = bf16[2,16,64,384]{3,2,1,0:T(8,128)(2,1)S(1)} all-to-all(bf16[2,16,64,384]{3,2,1,0:T(8,128)(2,1)S(1)} %broadcast_in_dim.69), channel_id=1, replica_groups=mesh['row_0'=2,'row_1'=8,'row_2'=2,'col'=16] {'row_2'}, dimensions={0} | all-to-all | bytes 3145728 | tf_op jit(solution)/shard_map/all_to_all | solution.py:13
  61.1 8.5 %while.30 = (s32[]{:T(128)}, f32[1024,256]{1,0:T(8,128)S(1)}, f32[1024]{0:T(1024)S(1)}, bf16[2048,128]{1,0:T(8,128)(2,1)S(1)}, bf16[1024,128]{1,0:T(8,128)(2,1)S...) while((s32[]{:T(128)}, f32[1024,256]{1,0:T(8,128)S(1)}, ...), condition=%wide.region_4.0_spmd.clone, body=%wide.region_2.4_spmd.clone.sunk | while | flops 203521792 | bytes 2629280 | solution.py:82
  70.7 8.3 %all-to-all-start.4 = ((bf16[16,64,256]{2,1,0:T(8,128)(2,1)}), bf16[16,64,256]{2,1,0:T(8,128)(2,1)S(1)}, u32[]{:S(2)}, u32[]{:S(2)}) async-start(bf16[16,64,256]{2,1,0:T(8,128)(2,1)} %bitcast.5), calls=%async_computation.4 | async-start | bytes 1048576 | tf_op jit(solution)/shard_map/all_to_all | solution.py:50
  79.0 15.8 %all-to-all-done.4 = bf16[16,64,256]{2,1,0:T(8,128)(2,1)S(1)} async-done(((bf16[16,64,256]{2,1,0:T(8,128)(2,1)}), bf16[16,64,256]{2,1,0:T(8,128)(2,1)S(1)}, u32[]{:S(2)}, u32[]{:S(2)}) %all-to-all-start.4) | async-done | bytes 524320 | tf_op jit(solution)/shard_map/all_to_all | solution.py:50
  95.4 4.1 %all-to-all-start = ((s32[16,1,64]{2,1,0:T(1,128)}), s32[16,1,64]{2,1,0:T(1,128)S(1)}, u32[]{:S(2)}, u32[]{:S(2)}) async-start(s32[16,1,64]{2,1,0:T(1,128)} %broadcast_in_dim.63), calls=%async_computation | async-start | bytes 16384 | tf_op jit(solution)/shard_map/all_to_all | solution.py:13
  99.7 6.5 %all-to-all-done = s32[16,1,64]{2,1,0:T(1,128)S(1)} async-done(((s32[16,1,64]{2,1,0:T(1,128)}), s32[16,1,64]{2,1,0:T(1,128)S(1)}, u32[]{:S(2)}, u32[]{:S(2)}) %all-to-all-start) | async-done | bytes 4128 | tf_op jit(solution)/shard_map/all_to_all | solution.py:13
  107.0 3.6 %all-to-all-start.5 = ((bf16[16,64,256]{2,1,0:T(8,128)(2,1)}), bf16[16,64,256]{2,1,0:T(8,128)(2,1)S(1)}, u32[]{:S(2)}, u32[]{:S(2)}) async-start(bf16[16,64,256]{2,1,0:T(8,128)(2,1)} %broadcast_in_dim.73), calls=%async_computation.5 | async-start | bytes 1048576 | tf_op jit(solution)/shard_map/all_to_all | solution.py:13
  110.7 4.3 %scatter_custom_fusion = s32[1024]{0:T(1024)S(1)} fusion(s32[1024]{0:T(1024)S(1)} %bitcast.70, s32[1024]{0:T(1024)S(1)} %iota.7, s32[]{:T(128)} %constant.128.clone.1), kind=kCustom, calls=%fused_computation.61 | custom fusion | bytes 4100 | tf_op jit(solution)/shard_map/scatter | solution.py:160
  115.2 10.9 %all-to-all-done.5 = bf16[16,64,256]{2,1,0:T(8,128)(2,1)S(1)} async-done(((bf16[16,64,256]{2,1,0:T(8,128)(2,1)}), bf16[16,64,256]{2,1,0:T(8,128)(2,1)S(1)}, u32[]{:S(2)}, u32[]{:S(2)}) %all-to-all-start.5) | async-done | bytes 524320 | tf_op jit(solution)/shard_map/all_to_all | solution.py:13
  127.0 26.6 %while.31 = (s32[]{:T(128)}, f32[1024,128]{1,0:T(8,128)S(1)}, bf16[2048,128]{1,0:T(8,128)(2,1)}, bf16[2048,256]{1,0:T(8,128)(2,1)}, bf16[1024,256]{1,0:T(8,128)(...) while((s32[]{:T(128)}, f32[1024,128]{1,0:T(8,128)S(1)}, ...), condition=%wide.region_10.11_spmd.clone, body=%wide.region_6.10_spmd.clone.sunk | while | flops 338885120 | bytes 6832329 | solution.py:119
  127.5 1.3 convert_reduce_fusion.6
  130.8 1.3 convert_reduce_fusion.6
  134.1 1.3 convert_reduce_fusion.6
  144.1 1.3 convert_reduce_fusion.6
  147.4 1.3 convert_reduce_fusion.6
  153.6 2.9 %gather_fusion = bf16[1024,128]{1,0:T(8,128)(2,1)S(1)} fusion(f32[1024,128]{1,0:T(8,128)S(1)} %get-tuple-element.267, s32[1024]{0:T(1024)S(1)} %fusion.34), kind=kCustom, calls=%fused_computation | custom fusion | bytes 528384 | tf_op jit(solution)/shard_map/jit(_take)/gather | solution.py:162
  156.7 11.7 %all_to_all.42 = bf16[16,64,128]{2,1,0:T(8,128)(2,1)S(1)} all-to-all(bf16[16,64,128]{2,1,0:T(8,128)(2,1)S(1)} %select_convert_fusion), channel_id=1, replica_groups=mesh['row_0'=2,'row_1'=8,'row_2'=2,'col'=16] {'col'}, dimensions={0} | all-to-all | bytes 524288 | tf_op jit(solution)/shard_map/all_to_all | solution.py:50
  168.4 9.0 %all-to-all-start.7 = ((bf16[32,64,128]{2,1,0:T(8,128)(2,1)}), bf16[32,64,128]{2,1,0:T(8,128)(2,1)S(1)}, u32[]{:S(2)}, u32[]{:S(2)}) async-start(bf16[32,64,128]{2,1,0:T(8,128)(2,1)} %bitcast.8), calls=%async_computation.7 | async-start | bytes 1048576 | tf_op jit(solution)/shard_map/all_to_all | solution.py:50
  178.0 17.4 %all-to-all-done.7 = bf16[32,64,128]{2,1,0:T(8,128)(2,1)S(1)} async-done(((bf16[32,64,128]{2,1,0:T(8,128)(2,1)}), bf16[32,64,128]{2,1,0:T(8,128)(2,1)S(1)}, u32[]{:S(2)}, u32[]{:S(2)}) %all-to-all-start.7) | async-done | bytes 524320 | tf_op jit(solution)/shard_map/all_to_all | solution.py:50
  (91 shorter events, 36.9 us)
Async XLA Ops:
  0.6 9.5 %copy-start = (f32[256,256]{1,0:T(8,128)S(1)}, f32[256,256]{1,0:T(8,128)}, u32[]{:S(2)}) copy-start(f32[256,256]{1,0:T(8,128)} %param.15) | copy-start | bytes 786436
  2.1 16.0 %all-to-all-start.3 = ((bf16[16,64,128]{2,1,0:T(8,128)(2,1)}), bf16[16,64,128]{2,1,0:T(8,128)(2,1)S(1)}, u32[]{:S(2)}, u32[]{:S(2)}) async-start(bf16[16,64,128]{2,1,0:T(8,128)(2,1)} %broadcast_in_dim.71), calls=%async_computation.3 | async-start | bytes 524288 | tf_op jit(solution)/shard_map/all_to_all | solution.py:13
  19.1 32.7 %all-to-all-start.1 = ((bf16[16,64,384]{2,1,0:T(8,128)(2,1)}), bf16[16,64,384]{2,1,0:T(8,128)(2,1)S(1)}, u32[]{:S(2)}, u32[]{:S(2)}) async-start(bf16[16,64,384]{2,1,0:T(8,128)(2,1)} %broadcast_in_dim.68), calls=%async_computation.1 | async-start | bytes 1572864 | tf_op jit(solution)/shard_map/all_to_all | solution.py:13
  69.6 1.2 copy-start.1
  69.6 25.2 %copy-start.4 = (s32[64]{0:T(128)S(1)}, s32[64]{0:T(128)}, u32[]{:S(2)}) copy-start(s32[64]{0:T(128)} %param.14) | copy-start | bytes 772
  69.6 30.0 %copy-start.2 = (bf16[64,256]{1,0:T(8,128)(2,1)S(1)}, bf16[64,256]{1,0:T(8,128)(2,1)}, u32[]{:S(2)}) copy-start(bf16[64,256]{1,0:T(8,128)(2,1)} %param.12) | copy-start | bytes 98308
  69.6 30.0 %copy-start.3 = (s32[64]{0:T(128)S(1)}, s32[64]{0:T(128)}, u32[]{:S(2)}) copy-start(s32[64]{0:T(128)} %param.13) | copy-start | bytes 772
  70.7 24.0 %all-to-all-start.4 = ((bf16[16,64,256]{2,1,0:T(8,128)(2,1)}), bf16[16,64,256]{2,1,0:T(8,128)(2,1)S(1)}, u32[]{:S(2)}, u32[]{:S(2)}) async-start(bf16[16,64,256]{2,1,0:T(8,128)(2,1)} %bitcast.5), calls=%async_computation.4 | async-start | bytes 1048576 | tf_op jit(solution)/shard_map/all_to_all | solution.py:50
  95.4 10.8 %all-to-all-start = ((s32[16,1,64]{2,1,0:T(1,128)}), s32[16,1,64]{2,1,0:T(1,128)S(1)}, u32[]{:S(2)}, u32[]{:S(2)}) async-start(s32[16,1,64]{2,1,0:T(1,128)} %broadcast_in_dim.63), calls=%async_computation | async-start | bytes 16384 | tf_op jit(solution)/shard_map/all_to_all | solution.py:13
  107.0 19.1 %all-to-all-start.5 = ((bf16[16,64,256]{2,1,0:T(8,128)(2,1)}), bf16[16,64,256]{2,1,0:T(8,128)(2,1)S(1)}, u32[]{:S(2)}, u32[]{:S(2)}) async-start(bf16[16,64,256]{2,1,0:T(8,128)(2,1)} %broadcast_in_dim.73), calls=%async_computation.5 | async-start | bytes 1048576 | tf_op jit(solution)/shard_map/all_to_all | solution.py:13
  168.4 27.1 %all-to-all-start.7 = ((bf16[32,64,128]{2,1,0:T(8,128)(2,1)}), bf16[32,64,128]{2,1,0:T(8,128)(2,1)S(1)}, u32[]{:S(2)}, u32[]{:S(2)}) async-start(bf16[32,64,128]{2,1,0:T(8,128)(2,1)} %bitcast.8), calls=%async_computation.7 | async-start | bytes 1048576 | tf_op jit(solution)/shard_map/all_to_all | solution.py:50
where the time goes:
time: 199 us; the launch traced here: 196 us
  waiting for transfers between devices  74.5 us (37%)
  starting transfers between devices  47.5 us (24%)
  matrix products  33.7 us (17%)
  blocking collectives  20.3 us (10%)
  local copies, waits for them, and re-layouts  13.1 us (7%)
  other arithmetic  5.52 us (3%)
    all_to_all x4, waiting for transfers between devices, sent_to_all(): return lax.all_to_all(copies, axis, split_axis=0, concat_axis=0, tiled=True)  41.4 us
    all_to_all x2, waiting for transfers between devices, summed_on_arrival(): lax.all_to_all(blocks, axis, split_axis=0, concat_axis=0, tiled=True)  33.2 us
    all_to_all x4, starting transfers between devices, sent_to_all(): return lax.all_to_all(copies, axis, split_axis=0, concat_axis=0, tiled=True)  30.3 us
    all_to_all x2, starting transfers between devices, summed_on_arrival(): lax.all_to_all(blocks, axis, split_axis=0, concat_axis=0, tiled=True)  17.3 us
    all_to_all x1, blocking collectives, summed_on_arrival(): lax.all_to_all(blocks, axis, split_axis=0, concat_axis=0, tiled=True)  11.7 us
    dot_general x8, matrix products, grad_advance(): lax.dot_general(adjoint, fitted_part, (((1,), (1,)), ((), ())), preferred...  10.6 us
    all_to_all x1, blocking collectives, sent_to_all(): return lax.all_to_all(copies, axis, split_axis=0, concat_axis=0, tiled=True)  8.66 us
    dot_general x8, matrix products, grad_advance(): lax.dot_general(weight, row_embed, (((0,), (0,)), ((), ())), preferred_el...  7.32 us
  transfers between devices with their start and end apart: 6, of which 6 were waited for; matrix products, arithmetic and copies ran while one was open for 4% of the time, Pallas kernels for 0%

commit v1 on v0

v1 whole, which is shorter than its diff:
```python
import jax
import jax.numpy as jnp
from jax import lax
from jax.experimental import pallas as pl
from jax.experimental.pallas import tpu as pltpu
from jax.sharding import PartitionSpec as P

MESH = pl.DeviceIdType.MESH
F32, BF16, I32 = jnp.float32, jnp.bfloat16, jnp.int32

OWN = 64
D = 128
E = 256
ROWS = 1024
COLS = 2048
ZREL = (0, 1, -1, 2, -2, 3, -3, 4)
ZSLOT = {z: k for k, z in enumerate(ZREL)}
ZSLOT[-4] = ZSLOT[4]
STEP = 256

NT = (((1,), (1,)), ((), ()))


def place():
    row, col = lax.axis_index("row"), lax.axis_index("col")
    return row // 16, (row // 2) % 8, row % 2, col // 4, col % 4


def at(h, z, c, x, l):
    return (h * 16 + z * 2 + c, x * 4 + l)


def pieces(wide):
    first = wide.astype(BF16).astype(F32)
    second = (wide - first).astype(BF16).astype(F32)
    third = (wide - first - second).astype(BF16).astype(F32)
    return first, second, third


def extended(embed, ones_first):
    wide = embed.astype(F32)
    squares = jnp.sum(wide * wide, axis=1, keepdims=True) * (-1.0 / D)
    a, b, c = pieces(squares)
    lane = lax.broadcasted_iota(I32, wide.shape, 1)
    at_parts = lane - 3 if ones_first else lane
    at_ones = lane if ones_first else lane - 3
    ones = jnp.where((at_ones >= 0) & (at_ones < 3), 1.0, 0.0)
    parts = jnp.where(at_parts == 0, a, jnp.where(at_parts == 1, b, jnp.where(at_parts == 2, c, ones)))
    return parts.astype(BF16)


def kernel(
    embed_ref, solution_ref, targets_ref, lengths_ref, ids_ref, epoch_ref,
    row_out, col_out,
    colb, cola, rowe, rowa, rowt, kst, facc, fitb, fit_x, fit_ys, fit_y,
    adjb, acr, idb, perm, cgf, cgx, cgr, cgs, cgd, rgf, rgb, rgs, rg_x, rg_ys, rg_y,
    ssem, rsem,
):
    h, z, c, x, l = place()
    count = [0]
    sent = []

    def send(src, dst, device):
        i = count[0]
        count[0] += 1
        copy = pltpu.make_async_remote_copy(
            src_ref=src, dst_ref=dst, send_sem=ssem.at[i], recv_sem=rsem.at[i],
            device_id=device, device_id_type=MESH,
        )
        copy.start()
        sent.append(copy)
        return copy

    core_peer = at(h, z, 1 - c, x, l)
    far_peer = at(1 - h, z, c, x, l)
    z_peer = lambda d: at(h, (z + d + 8) % 8, c, x, l)
    x_peer = lambda d: at(h, z, c, (x + d + 4) % 4, l)
    l_peer = lambda d: at(h, z, c, x, (l + d + 4) % 4)

    barrier = pltpu.get_barrier_semaphore()
    peers = [core_peer, far_peer, z_peer(1), z_peer(-1)]
    peers += [x_peer(d) for d in (1, 2, 3)] + [l_peer(d) for d in (1, 2, 3)]
    for peer in peers:
        pl.semaphore_signal(barrier, inc=1, device_id=peer, device_id_type=MESH)

    def block(slot):
        return pl.ds(slot * OWN, OWN)

    fitted = jnp.dot(
        solution_ref[...], epoch_ref[...], precision=lax.Precision.HIGHEST, preferred_element_type=F32
    )
    colb[0:OWN, 0:D] = embed_ref[...]
    colb[0:OWN, D : D + E] = fitted.astype(BF16)
    rowe[0:OWN, :] = embed_ref[...]
    ids = ids_ref[...]
    idb[0] = jnp.broadcast_to(jnp.concatenate([ids, ids], axis=1), (8, 128))
    pl.semaphore_wait(barrier, len(peers))

    def slot_of(far, zrel, other):
        return far * 16 + ZSLOT[zrel] * 2 + other

    came = {}

    def pass_on(far, zrel):
        src = colb.at[block(slot_of(far, zrel, 0)), :]
        most_up, most_down = (4, 3) if far == 0 else (3, 4)
        if zrel <= 0 and -zrel < most_up:
            came[far, zrel - 1] = send(src, colb.at[block(slot_of(far, zrel - 1, 0)), :], z_peer(1))
        if 0 <= zrel < most_down:
            came[far, zrel + 1] = send(src, colb.at[block(slot_of(far, zrel + 1, 0)), :], z_peer(-1))
        came[far, zrel, "core"] = send(src, colb.at[block(slot_of(far, zrel, 1)), :], core_peer)

    far_copy = send(colb.at[block(0), :], colb.at[block(16), :], far_peer)
    pass_on(0, 0)

    def gather_rows(ref):
        along_l = [send(ref(0), ref(d), l_peer(-d)) for d in (1, 2, 3)]
        along_x = [send(ref(0), ref(d * 4), x_peer(-d)) for d in (1, 2, 3)]

        def spread():
            for d, copy in zip((1, 2, 3), along_l):
                copy.wait_recv()
                along_x.extend(send(ref(d), ref(e * 4 + d), x_peer(-e)) for e in (1, 2, 3))

        def finish():
            for copy in along_x:
                copy.wait_recv()

        return spread, finish

    spread_rows, finish_rows = gather_rows(lambda s: rowe.at[block(s), :])
    spread_ids, finish_ids = gather_rows(lambda s: idb.at[s])

    def arrive(far, zrel):
        came[far, zrel].wait_recv()
        pass_on(far, zrel)

    arrive(0, -1), arrive(0, 1)
    spread_rows()
    arrive(0, -2), arrive(0, 2)
    far_copy.wait_recv()
    pass_on(1, 0)
    arrive(0, -3), arrive(0, 3)
    arrive(0, -4)
    spread_ids()
    finish_rows()

    rowe_all = rowe[...]
    rowa[:, 0:D] = (rowe_all.astype(F32) * (1.0 / 64)).astype(BF16)
    rowa[:, D:] = extended(rowe_all, True)

    arrive(1, -1), arrive(1, 1)
    arrive(1, -2), arrive(1, 2)
    arrive(1, -3), arrive(1, 3)
    arrive(1, 4)
    for far in (0, 1):
        for zrel in ZREL:
            key = (far, -4, "core") if (far == 0 and zrel == 4) else (far, zrel, "core")
            came[key].wait_recv()

    @pl.loop(0, COLS // STEP)
    def _(i):
        rows = pl.ds(i * STEP, STEP)
        embed = colb[rows, 0:D]
        cola[rows, 0:D] = embed
        cola[rows, D:] = extended(embed, False)

    def fit_rows(chunk):
        rows = pl.ds(chunk * STEP, STEP)
        facc[...] = jnp.zeros_like(facc)

        @pl.loop(0, COLS // STEP)
        def _(i):
            cols = pl.ds(i * STEP, STEP)
            power = lax.dot_general(rowa[rows, :], cola[cols, :], NT, preferred_element_type=F32)
            kern = jnp.exp(power)
            kst[i, rows, :] = kern
            facc[...] += jnp.dot(kern.astype(BF16), colb[cols, D : D + E], preferred_element_type=F32)

    fit_copies = {}
    for d in (2, 1, 3):
        fit_rows(d)
        fitb[pl.ds((d - 1) * STEP, STEP), :] = facc[...].astype(BF16)
        fit_copies[d] = send(fitb.at[pl.ds((d - 1) * STEP, STEP), :], fit_x.at[d - 1], x_peer(d))
    fit_rows(0)
    for d in (2, 1, 3):
        fit_copies[d].wait_recv()
        facc[...] += fit_x[d - 1].astype(F32)
    y_copies = []
    for d in (1, 2, 3):
        fit_ys[d - 1] = facc[pl.ds(d * OWN, OWN), :].astype(BF16)
        y_copies.append(send(fit_ys.at[d - 1], fit_y.at[d - 1], l_peer(d)))

    rowt[...] = rowa[...].T
    finish_ids()
    lane = lax.broadcasted_iota(I32, (1, 128), 1)

    @pl.loop(0, 8)
    def _(i):
        both = jnp.where(lane < OWN, idb[2 * i, 0:1, :], idb[2 * i + 1, 0:1, :])
        across_x = (((both >> 8) & 3) - x) & 3
        across_l = (((both >> 6) & 3) - l) & 3
        goal = across_x * 256 + across_l * OWN + (both & (OWN - 1))
        seat = lax.broadcasted_iota(I32, (ROWS, 128), 0)
        perm[i] = jnp.where(seat == goal, 1.0, 0.0).astype(BF16)

    diagonal = lax.broadcasted_iota(I32, (OWN, OWN), 0) == lax.broadcasted_iota(I32, (OWN, OWN), 1)
    spans = jnp.broadcast_to(lengths_ref[...].astype(F32), (OWN, OWN))
    span = jnp.sum(jnp.where(diagonal, spans, 0.0), axis=1, keepdims=True)
    epoch = lax.broadcasted_iota(I32, (OWN, E), 1).astype(F32)

    total = facc[0:OWN, :]
    for d in (1, 2, 3):
        y_copies[d - 1].wait_recv()
        total += fit_y[d - 1].astype(F32)
    adjoint = jnp.where(epoch < span, targets_ref[...].astype(F32) - total, 0.0).astype(BF16)
    adjb[0:OWN, :] = adjoint
    spread_adjoint, finish_adjoint = gather_rows(lambda s: adjb.at[block(s), :])
    spread_adjoint()
    acr[...] = jnp.zeros_like(acr)
    finish_adjoint()

    @pl.loop(0, COLS // STEP)
    def _(i):
        cols = pl.ds(i * STEP, STEP)
        down = jnp.zeros((2 * D, STEP), F32)
        for r in range(ROWS // STEP):
            rows = slice(r * STEP, (r + 1) * STEP)
            link = lax.dot_general(adjb[rows, :], colb[cols, D : D + E], NT, preferred_element_type=F32)
            weight = (link * kst[i, rows, :]).astype(BF16)
            acr[rows, :] += jnp.dot(weight, cola[cols, :], preferred_element_type=F32)
            down += jnp.dot(rowt[:, rows], weight, preferred_element_type=F32)
        turned = down.T
        grad = turned[:, 0:D] * 64.0 - cola[cols, 0:D].astype(F32) * turned[:, D : D + 1]
        for s in range(2):
            mine = grad[2 * s * OWN : (2 * s + 1) * OWN]
            other = grad[(2 * s + 1) * OWN : (2 * s + 2) * OWN]
            cgf[2 * i + s] = mine
            cgx[2 * i + s] = other.astype(BF16)

    core_copy = send(cgx, cgr, core_peer)

    sums = acr[:, D + 3 : D + 4]
    rgb[...] = (acr[:, 0:D] - rowe[...].astype(F32) * sums).astype(BF16)
    placed = jnp.zeros((ROWS, D), F32)
    for i in range(8):
        placed += jnp.dot(perm[i], rgb[i * 128 : (i + 1) * 128, :], preferred_element_type=F32)
    rgf[...] = placed[0:STEP]
    rgs[...] = placed[STEP:].astype(BF16)
    rg_copies = {}
    for d in (2, 1, 3):
        rg_copies[d] = send(rgs.at[pl.ds((d - 1) * STEP, STEP), :], rg_x.at[d - 1], x_peer(d))

    core_copy.wait_recv()
    col_copies = []
    for k in (7, 15, 13, 14, 11, 12, 9, 10, 5, 6, 3, 4, 1, 2, 8):
        far, zrel = k // 8, ZREL[k % 8]
        cgs[k] = (cgf[k] + cgr[k].astype(F32)).astype(BF16)
        owner = at((h + far) % 2, (z + zrel + 8) % 8, c, x, l)
        col_copies.append((k, send(cgs.at[k], cgd.at[k], owner)))

    for d in (2, 1, 3):
        rg_copies[d].wait_recv()
        rgf[...] += rg_x[d - 1].astype(F32)
    last = []
    for d in (1, 2, 3):
        rg_ys[d - 1] = rgf[pl.ds(d * OWN, OWN), :].astype(BF16)
        last.append(send(rg_ys.at[d - 1], rg_y.at[d - 1], l_peer(d)))
    row_total = rgf[0:OWN, :]
    for d in (1, 2, 3):
        last[d - 1].wait_recv()
        row_total += rg_y[d - 1].astype(F32)
    row_out[...] = row_total * (2.0 / D)

    col_total = cgf[0] + cgr[0].astype(F32)
    for k, copy in col_copies:
        copy.wait_recv()
        col_total += cgd[k].astype(F32)
    col_out[...] = col_total * (2.0 / D)
    for copy in sent:
        copy.wait_send()


def per_device(curve_embed, solution, targets, lengths, slot_curve, epoch_kernel):
    vmem = pl.BlockSpec(memory_space=pltpu.VMEM)
    scratch = [
        ((COLS, D + E), BF16), ((COLS, 2 * D), BF16), ((ROWS, D), BF16), ((ROWS, 2 * D), BF16),
        ((2 * D, ROWS), BF16), ((COLS // STEP, ROWS, STEP), F32), ((STEP, E), F32), ((3 * STEP, E), BF16),
        ((3, STEP, E), BF16), ((3, OWN, E), BF16), ((3, OWN, E), BF16),
        ((ROWS, E), BF16), ((ROWS, 2 * D), F32), ((16, 8, 128), I32), ((8, ROWS, 128), BF16),
        ((16, OWN, D), F32), ((16, OWN, D), BF16), ((16, OWN, D), BF16), ((16, OWN, D), BF16),
        ((16, OWN, D), BF16), ((STEP, D), F32), ((ROWS, D), BF16), ((3 * STEP, D), BF16),
        ((3, STEP, D), BF16), ((3, OWN, D), BF16), ((3, OWN, D), BF16),
    ]
    return pl.pallas_call(
        kernel,
        out_shape=(jax.ShapeDtypeStruct((OWN, D), F32), jax.ShapeDtypeStruct((OWN, D), F32)),
        in_specs=[vmem] * 6,
        out_specs=(vmem, vmem),
        scratch_shapes=[pltpu.VMEM(s, t) for s, t in scratch]
        + [pltpu.SemaphoreType.DMA((128,)), pltpu.SemaphoreType.DMA((128,))],
        compiler_params=pltpu.CompilerParams(
            collective_id=0, has_side_effects=True, vmem_limit_bytes=56 * 2**20
        ),
        name="tile",
    )(curve_embed, solution, targets, lengths.reshape(1, OWN), slot_curve.reshape(1, OWN), epoch_kernel)


def solution(mesh):
    both = ("row", "col")
    return jax.shard_map(
        per_device,
        mesh=mesh,
        in_specs=(P(both, None), P(both, None), P(both, None), P(both), P(both), P()),
        out_specs=(P(both, None), P(both, None)),
        check_vma=False,
    )
```

time: 199 us -> 95.2 us (0.48); the launches traced: 196 us -> 95 us
  Pallas kernels: 0 us -> 92.4 us
  waiting for transfers between devices: 74.5 us -> 0 us
  starting transfers between devices: 47.5 us -> 0 us
  matrix products: 33.7 us -> 0 us
  blocking collectives: 20.3 us -> 0 us
  local copies, waits for them, and re-layouts: 13.1 us -> 2 us
  other arithmetic: 5.52 us -> 0 us
    pallas_call x0 -> x1, Pallas kernels: none -> 92.4 us  [per_device(): pl.pallas_call(kernel, out_shape=(jax.ShapeDtypeStruct((OWN, D), F32), ja...]
    all_to_all x6 -> x0, waiting for transfers between devices: 74.5 us -> none  [the longest x4 41.4 us: sent_to_all(): return lax.all_to_all(copies, axis, split_axis=0, concat_axis=0, tiled=True)]
    all_to_all x6 -> x0, starting transfers between devices: 47.5 us -> none  [the longest x4 30.3 us: sent_to_all(): return lax.all_to_all(copies, axis, split_axis=0, concat_axis=0, tiled=True)]
    dot_general x41 -> x0, matrix products: 33.7 us -> none  [the longest x8 10.6 us: grad_advance(): lax.dot_general(adjoint, fitted_part, (((1,), (1,)), ((), ())), preferred...]
    all_to_all x2 -> x0, blocking collectives: 20.3 us -> none  [the longest x1 11.7 us: summed_on_arrival(): lax.all_to_all(blocks, axis, split_axis=0, concat_axis=0, tiled=True)]
    broadcast_in_dim x7 -> x0, local copies, waits for them, and re-layouts: 5.17 us -> none  [the longest x5 4.21 us: sent_to_all(): copies = jnp.broadcast_to(x, (lax.axis_size(axis), *x.shape))]
    scatter x1 -> x0, local copies, waits for them, and re-layouts: 4.31 us -> none  [per_device(): inverse = jnp.zeros((group_size,), jnp.int32).at[local_curve].set(jnp.ara...]
    gather x1 -> x0, local copies, waits for them, and re-layouts: 2.88 us -> none  [per_device(): reordered = jnp.take(row_sum, inverse, axis=0)]
  transfers between devices with their start and end apart: 6 -> 0, of which waited for: 6 -> 0; matrix products, arithmetic and copies ran while one was open for 4% -> 0% of each run, Pallas kernels for 0% -> 0%
where the time goes in v1:
time: 95.2 us; the launch traced here: 95 us
  Pallas kernels  92.4 us (97%)
  local copies, waits for them, and re-layouts  2 us (2%)
    pallas_call x1, Pallas kernels, per_device(): pl.pallas_call(kernel, out_shape=(jax.ShapeDtypeStruct((OWN, D), F32), ja...  92.4 us
    unnamed x4, local copies, waits for them, and re-layouts  2 us

profile of v1, /device:TPU:1, one launch (start us, length us, event | category | flops | bytes accessed | tf_op | source)
XLA Modules:
  0.0 95.0 jit_solution(8809305169694162306)
XLA Ops:
  0.6 92.4 %tile.1 = (f32[64,128]{1,0:T(8,128)}, f32[64,128]{1,0:T(8,128)}) custom-call(bf16[64,128]{1,0:T(8,128)(2,1)} %embed_ref.1, f32[64,256]{1,0:T(8,128)} %solution_ref.1, bf16[64,256]{1,0:T(8,128)(2,1)} %targets_ref.1, s32[1,64]{1,0:T(1,128)} %bitcast.2, s32[1,64]{1,0:T(1,128)} %bitcast.3, f32[256,256]{1,0:T(8,128)} %epoch_ref.1), custom_call_target="tpu_custom_call" | custom-call | tf_op jit(solution)/shard_map/tile/pallas_call | solution.py:295
  93.0 0.0 copy-start
  93.0 1.4 %copy.10 = f32[64,128]{1,0:T(8,128)} copy(f32[64,128]{1,0:T(8,128)} %get-tuple-element.4) | data formatting | bytes 65536
  94.4 0.0 copy-done
  94.4 0.6 copy.11
Async XLA Ops:
  93.0 1.4 %copy-start = (f32[64,128]{1,0:T(8,128)S(1)}, f32[64,128]{1,0:T(8,128)}, u32[]{:S(2)}) copy-start(f32[64,128]{1,0:T(8,128)} %get-tuple-element.5) | copy-start | bytes 98308

commit v2 on v1

v2 whole, which is shorter than its diff:
```python
import jax
import jax.numpy as jnp
from jax import lax
from jax.experimental import pallas as pl
from jax.experimental.pallas import tpu as pltpu
from jax.sharding import PartitionSpec as P

MESH = pl.DeviceIdType.MESH
F32, BF16, I32 = jnp.float32, jnp.bfloat16, jnp.int32

OWN = 64
D = 128
E = 256
ROWS = 1024
COLS = 2048
ZREL = (0, 1, -1, 2, -2, 3, -3, 4)
ZSLOT = {z: k for k, z in enumerate(ZREL)}
ZSLOT[-4] = ZSLOT[4]
STEP = 256
TURNED = 144

NT = (((1,), (1,)), ((), ()))


def place():
    row, col = lax.axis_index("row"), lax.axis_index("col")
    return row // 16, (row // 2) % 8, row % 2, col // 4, col % 4


def at(h, z, c, x, l):
    return (h * 16 + z * 2 + c, x * 4 + l)


def pieces(wide):
    first = wide.astype(BF16).astype(F32)
    second = (wide - first).astype(BF16).astype(F32)
    third = (wide - first - second).astype(BF16).astype(F32)
    return first, second, third


def extended(embed, ones_first):
    wide = embed.astype(F32)
    squares = jnp.sum(wide * wide, axis=1, keepdims=True) * (-1.0 / D)
    a, b, c = pieces(squares)
    lane = lax.broadcasted_iota(I32, wide.shape, 1)
    at_parts = lane - 3 if ones_first else lane
    at_ones = lane if ones_first else lane - 3
    ones = jnp.where((at_ones >= 0) & (at_ones < 3), 1.0, 0.0)
    parts = jnp.where(at_parts == 0, a, jnp.where(at_parts == 1, b, jnp.where(at_parts == 2, c, ones)))
    return parts.astype(BF16)


def kernel(
    embed_hbm, solution_hbm, targets_hbm, lengths_hbm, ids_hbm, epoch_hbm,
    row_out, col_out,
    embed_ref, solution_ref, targets_ref, lengths_ref, ids_ref, epoch_ref,
    colb, cola, colt, rowe, rowa, rowt, kst, facc, fitb, fit_x, fit_s, fit_y,
    adjb, acr, idb, perm, dnt, gtb, cgf, cgx, cgr, cgs, cgd, rgb, rgf, rgs, rg_x, rg_s, rg_y,
    ssem, rsem, lsem,
):
    h, z, c, x, l = place()
    count = [0]
    sent = []

    def send(src, dst, device):
        i = count[0]
        count[0] += 1
        copy = pltpu.make_async_remote_copy(
            src_ref=src, dst_ref=dst, send_sem=ssem.at[i], recv_sem=rsem.at[i],
            device_id=device, device_id_type=MESH,
        )
        copy.start()
        sent.append(copy)
        return copy

    core_peer = at(h, z, 1 - c, x, l)
    far_peer = at(1 - h, z, c, x, l)
    z_peer = lambda d: at(h, (z + d + 8) % 8, c, x, l)
    plane_peer = lambda dx, dl: at(h, z, c, (x + dx + 4) % 4, (l + dl + 4) % 4)

    barrier = pltpu.get_barrier_semaphore()
    peers = [core_peer, far_peer] + [z_peer(d) for d in (1, -1, 2, -2)]
    peers += [plane_peer(d, 0) for d in (1, 2, 3)] + [plane_peer(0, d) for d in (1, 2, 3)]
    for peer in peers:
        pl.semaphore_signal(barrier, inc=1, device_id=peer, device_id_type=MESH)

    loads = [
        pltpu.make_async_copy(src, dst, lsem.at[i])
        for i, (src, dst) in enumerate([
            (solution_hbm, solution_ref), (epoch_hbm, epoch_ref), (embed_hbm, embed_ref),
            (ids_hbm, ids_ref), (targets_hbm, targets_ref), (lengths_hbm, lengths_ref),
        ])
    ]
    for load in loads:
        load.start()
    for load in loads[:4]:
        load.wait()

    def block(slot):
        return pl.ds(slot * OWN, OWN)

    fitted = jnp.dot(
        solution_ref[...], epoch_ref[...], precision=lax.Precision.HIGHEST, preferred_element_type=F32
    )
    colb[0:OWN, 0:D] = embed_ref[...]
    colb[0:OWN, D : D + E] = fitted.astype(BF16)
    rowe[0:OWN, :] = embed_ref[...]
    ids = ids_ref[...]
    idb[0] = jnp.broadcast_to(jnp.concatenate([ids, ids], axis=1), (8, 128))
    pl.semaphore_wait(barrier, len(peers))

    def slot_of(far, zrel, other):
        return far * 16 + ZSLOT[zrel] * 2 + other

    came = {}

    def forward(far, zrel, steps):
        for step in steps:
            goal = zrel - step
            came[far, ZSLOT[goal]] = send(
                colb.at[block(slot_of(far, zrel, 0)), :], colb.at[block(slot_of(far, goal, 0)), :], z_peer(step)
            )

    def share(far, zrel):
        came[far, ZSLOT[zrel], "core"] = send(
            colb.at[block(slot_of(far, zrel, 0)), :], colb.at[block(slot_of(far, zrel, 1)), :], core_peer
        )

    def arrive(far, zrel):
        came[far, ZSLOT[zrel]].wait_recv()
        share(far, zrel)

    far_copy = send(colb.at[block(0), :], colb.at[block(16), :], far_peer)
    forward(0, 0, (1, -1, 2, -2))
    share(0, 0)

    def gather_rows(ref):
        along_l = [send(ref(0), ref(d), plane_peer(0, -d)) for d in (1, 2, 3)]
        along_x = [send(ref(0), ref(d * 4), plane_peer(-d, 0)) for d in (2, 1, 3)]

        def spread():
            for d, copy in zip((1, 2, 3), along_l):
                copy.wait_recv()
                along_x.extend(send(ref(d), ref(e * 4 + d), plane_peer(-e, 0)) for e in (2, 1, 3))

        def finish():
            for copy in along_x:
                copy.wait_recv()

        return spread, finish

    spread_rows, finish_rows = gather_rows(lambda s: rowe.at[block(s), :])

    arrive(0, -1), arrive(0, 1)
    arrive(0, -2)
    forward(0, -2, (2, 1))
    arrive(0, 2)
    forward(0, 2, (-1,))
    far_copy.wait_recv()
    forward(1, 0, (-2, 2, -1, 1))
    share(1, 0)
    spread_rows()
    arrive(0, -3), arrive(0, 3), arrive(0, 4)
    arrive(1, 2)
    forward(1, 2, (-2, -1))
    arrive(1, -2)
    forward(1, -2, (1,))
    arrive(1, -1), arrive(1, 1)

    finish_rows()
    id_copies = [send(idb.at[0], idb.at[s], plane_peer(-(s // 4), -(s % 4))) for s in range(1, 16)]
    rowe_all = rowe[...]
    rowa[:, 0:D] = (rowe_all.astype(F32) * (1.0 / 64)).astype(BF16)
    rowa[:, D:] = extended(rowe_all, True)

    def columns_in(far):
        for k in range(8):
            came[far, k, "core"].wait_recv()
        cols = slice(far * COLS // 2, (far + 1) * COLS // 2)
        embed = colb[cols, 0:D]
        cola[cols, 0:D] = embed
        cola[cols, D:] = extended(embed, False)

    def fit_rows(far, rows, total):
        for i in range(far * 4, far * 4 + 4):
            cols = slice(i * STEP, (i + 1) * STEP)
            power = lax.dot_general(rowa[rows, :], cola[cols, :], NT, preferred_element_type=F32)
            kern = jnp.exp(power)
            kst[i, rows, :] = kern
            part = jnp.dot(kern.astype(BF16), colb[cols, D : D + E], preferred_element_type=F32)
            total = part if total is None else total + part
        return total

    columns_in(0)

    @pl.loop(0, ROWS // STEP)
    def _(r):
        rows = pl.ds(r * STEP, STEP)
        facc[rows, :] = fit_rows(0, rows, None)

    arrive(1, -3), arrive(1, 3), arrive(1, 4)
    columns_in(1)

    def scatter(d, ref, got):
        return {r: send(ref.at[block(4 * d + r), :], got.at[4 * (d - 1) + r], plane_peer(d, 0)) for r in (2, 1, 3, 0)}

    def reduce_rows(copies, mine, got, going, ends):
        last = []
        for r in (2, 1, 3, 0):
            for d in (2, 1, 3):
                copies[d][r].wait_recv()
            rows = block(r)
            mine[rows, :] += sum(got[4 * d + r].astype(F32) for d in range(3))
            if r:
                going[r - 1] = mine[rows, :].astype(BF16)
                last.append(send(going.at[r - 1], ends.at[r - 1], plane_peer(0, r)))
        return last

    fit_copies = {}
    for d in (2, 1, 3, 0):
        rows = slice(d * STEP, (d + 1) * STEP)
        total = fit_rows(1, rows, facc[rows, :])
        if d:
            fitb[rows, :] = total.astype(BF16)
            fit_copies[d] = scatter(d, fitb, fit_x)
        else:
            facc[rows, :] = total

    fit_last = reduce_rows(fit_copies, facc, fit_x, fit_s, fit_y)

    rowt[...] = rowa[...].T[0:TURNED]
    colt[...] = colb[:, 0:D].T
    acr[...] = jnp.zeros_like(acr)
    for copy in id_copies:
        copy.wait_recv()
    lane = lax.broadcasted_iota(I32, (1, 128), 1)

    @pl.loop(0, 8)
    def _(i):
        both = jnp.where(lane < OWN, idb[2 * i, 0:1, :], idb[2 * i + 1, 0:1, :])
        across_x = (((both >> 8) & 3) - x) & 3
        across_l = (((both >> 6) & 3) - l) & 3
        goal = across_x * 256 + across_l * OWN + (both & (OWN - 1))
        seat = lax.broadcasted_iota(I32, (ROWS, 128), 0)
        perm[i // 2, :, pl.ds(pl.multiple_of((i % 2) * 128, 128), 128)] = jnp.where(seat == goal, 1.0, 0.0).astype(BF16)

    for load in loads[4:]:
        load.wait()
    diagonal = lax.broadcasted_iota(I32, (OWN, OWN), 0) == lax.broadcasted_iota(I32, (OWN, OWN), 1)
    spans = jnp.broadcast_to(lengths_ref[...].astype(F32), (OWN, OWN))
    span = jnp.sum(jnp.where(diagonal, spans, 0.0), axis=1, keepdims=True)
    epoch = lax.broadcasted_iota(I32, (OWN, E), 1).astype(F32)

    total = facc[0:OWN, :]
    for r, copy in enumerate(fit_last):
        copy.wait_recv()
    total += sum(fit_y[r].astype(F32) for r in range(3))
    adjoint = jnp.where(epoch < span, targets_ref[...].astype(F32) - total, 0.0).astype(BF16)
    adjb[0:OWN, :] = adjoint
    spread_adjoint, finish_adjoint = gather_rows(lambda s: adjb.at[block(s), :])
    spread_adjoint()

    def grad_rows(i, rows):
        cols = pl.ds(i * STEP, STEP)
        link = lax.dot_general(adjb[rows, :], colb[cols, D : D + E], NT, preferred_element_type=F32)
        weight = (link * kst[i, rows, :]).astype(BF16)
        acr[rows, :] += jnp.dot(weight, cola[cols, :], preferred_element_type=F32)
        return jnp.dot(rowt[:, rows], weight, preferred_element_type=F32)

    @pl.loop(0, COLS // STEP, step=2)
    def _(i):
        for j in (i, i + 1):
            dnt[j] = grad_rows(j, slice(0, STEP))

    finish_adjoint()

    col_copies = []
    swaps = {}

    def add_cores(i):
        swaps[i].wait_recv()
        for k in (2 * i + 1, 2 * i):
            if k == 0:
                continue
            far, zrel = k // 8, ZREL[k % 8]
            cgs[k] = (cgf[k] + cgr[k].astype(F32)).astype(BF16)
            owner = at((h + far) % 2, (z + zrel + 8) % 8, c, x, l)
            col_copies.append((k, send(cgs.at[k], cgd.at[k], owner)))

    def turn(i, n):
        turned = gtb[n % 2].T
        for s in range(2):
            cgf[2 * i + s] = turned[2 * s * OWN : (2 * s + 1) * OWN]
            cgx[2 * i + s] = turned[(2 * s + 1) * OWN : (2 * s + 2) * OWN].astype(BF16)

    def swap(i):
        pair = pl.ds(2 * i, 2)
        swaps[i] = send(cgx.at[pair], cgr.at[pair], core_peer)

    order = (7, 6, 5, 3, 4, 2, 1, 0)
    for n, i in enumerate(order):
        down = dnt[i] + grad_rows(i, slice(STEP, ROWS))
        gtb[n % 2] = down[0:D] * 64.0 - colt[:, i * STEP : (i + 1) * STEP].astype(F32) * down[D : D + 1]
        if n:
            turn(order[n - 1], n - 1)
            swap(order[n - 1])
        if n > 1:
            add_cores(order[n - 2])
    turn(0, 7)
    swap(0)

    sums = acr[:, D + 3 : D + 4]
    rgb[...] = (acr[:, 0:D] - rowe[...].astype(F32) * sums).astype(BF16)

    def placed(d):
        rows = slice(d * STEP, (d + 1) * STEP)
        return sum(
            jnp.dot(perm[i, rows, :], rgb[i * STEP : (i + 1) * STEP, :], preferred_element_type=F32) for i in range(4)
        )

    row_copies = {}
    for d in (2, 1, 3):
        rgs[d * STEP : (d + 1) * STEP, :] = placed(d).astype(BF16)
        row_copies[d] = scatter(d, rgs, rg_x)
    rgf[...] = placed(0)
    add_cores(order[-2])
    add_cores(order[-1])

    row_last = reduce_rows(row_copies, rgf, rg_x, rg_s, rg_y)
    for copy in row_last:
        copy.wait_recv()
    row_total = rgf[0:OWN, :] + sum(rg_y[r].astype(F32) for r in range(3))
    row_out[...] = row_total * (2.0 / D)

    for k, copy in col_copies:
        copy.wait_recv()
    col_total = cgf[0] + cgr[0].astype(F32)
    for k, copy in col_copies:
        col_total += cgd[k].astype(F32)
    col_out[...] = col_total * (2.0 / D)
    for copy in sent:
        copy.wait_send()


def per_device(curve_embed, solution, targets, lengths, slot_curve, epoch_kernel):
    vmem = pl.BlockSpec(memory_space=pltpu.VMEM)
    scratch = [
        ((OWN, D), BF16), ((OWN, E), F32), ((OWN, E), BF16), ((1, OWN), I32), ((1, OWN), I32), ((E, E), F32),
        ((COLS, D + E), BF16), ((COLS, 2 * D), BF16), ((D, COLS), BF16), ((ROWS, D), BF16), ((ROWS, 2 * D), BF16),
        ((TURNED, ROWS), BF16), ((COLS // STEP, ROWS, STEP), F32), ((ROWS, E), F32), ((ROWS, E), BF16),
        ((12, OWN, E), BF16), ((3, OWN, E), BF16), ((3, OWN, E), BF16),
        ((ROWS, E), BF16), ((ROWS, 2 * D), F32), ((16, 8, 128), I32), ((4, ROWS, STEP), BF16),
        ((COLS // STEP, TURNED, STEP), F32), ((2, D, STEP), F32),
        ((16, OWN, D), F32), ((16, OWN, D), BF16), ((16, OWN, D), BF16), ((16, OWN, D), BF16),
        ((16, OWN, D), BF16), ((ROWS, D), BF16), ((STEP, D), F32), ((ROWS, D), BF16),
        ((12, OWN, D), BF16), ((3, OWN, D), BF16), ((3, OWN, D), BF16),
    ]
    return pl.pallas_call(
        kernel,
        out_shape=(jax.ShapeDtypeStruct((OWN, D), F32), jax.ShapeDtypeStruct((OWN, D), F32)),
        in_specs=[pl.BlockSpec(memory_space=pl.ANY)] * 6,
        out_specs=(vmem, vmem),
        scratch_shapes=[pltpu.VMEM(s, t) for s, t in scratch]
        + [pltpu.SemaphoreType.DMA((160,)), pltpu.SemaphoreType.DMA((160,)), pltpu.SemaphoreType.DMA((6,))],
        compiler_params=pltpu.CompilerParams(
            collective_id=0, has_side_effects=True, vmem_limit_bytes=56 * 2**20
        ),
        name="tile",
    )(curve_embed, solution, targets, lengths.reshape(1, OWN), slot_curve.reshape(1, OWN), epoch_kernel)


def solution(mesh):
    both = ("row", "col")
    return jax.shard_map(
        per_device,
        mesh=mesh,
        in_specs=(P(both, None), P(both, None), P(both, None), P(both), P(both), P()),
        out_specs=(P(both, None), P(both, None)),
        check_vma=False,
    )
```

time: 95.2 us -> 74.3 us (0.78)
  Pallas kernels: 92.4 us -> 71.4 us
    pallas_call x1, Pallas kernels: 92.4 us -> 71.4 us  [per_device(): pl.pallas_call(kernel, out_shape=(jax.ShapeDtypeStruct((OWN, D), F32), ja...]
where the time goes in v2:
time: 74.3 us; the launch traced here: 74 us
  Pallas kernels  71.4 us (96%)
  local copies, waits for them, and re-layouts  2 us (3%)
    pallas_call x1, Pallas kernels, per_device(): pl.pallas_call(kernel, out_shape=(jax.ShapeDtypeStruct((OWN, D), F32), ja...  71.4 us
    unnamed x4, local copies, waits for them, and re-layouts  2 us

profile of v2, /device:TPU:1, one launch (start us, length us, event | category | flops | bytes accessed | tf_op | source)
XLA Modules:
  0.0 74.0 jit_solution(15627547030421983773)
XLA Ops:
  0.6 71.4 %tile.1 = (f32[64,128]{1,0:T(8,128)}, f32[64,128]{1,0:T(8,128)}) custom-call(bf16[64,128]{1,0:T(8,128)(2,1)} %embed_hbm.1, f32[64,256]{1,0:T(8,128)} %solution_hbm.1, bf16[64,256]{1,0:T(8,128)(2,1)} %targets_hbm.1, s32[1,64]{1,0:T(1,128)} %bitcast.2, s32[1,64]{1,0:T(1,128)} %bitcast.3, f32[256,256]{1,0:T(8,128)} %epoch_hbm.1), custom_call_target="tpu_custom_call" | custom-call | tf_op jit(solution)/shard_map/tile/pallas_call | solution.py:358
  72.0 0.0 copy-start
  72.0 1.4 %copy.10 = f32[64,128]{1,0:T(8,128)} copy(f32[64,128]{1,0:T(8,128)} %get-tuple-element.4) | data formatting | bytes 65536
  73.4 0.0 copy-done
  73.4 0.6 copy.11
Async XLA Ops:
  72.0 1.4 %copy-start = (f32[64,128]{1,0:T(8,128)S(1)}, f32[64,128]{1,0:T(8,128)}, u32[]{:S(2)}) copy-start(f32[64,128]{1,0:T(8,128)} %get-tuple-element.5) | copy-start | bytes 98308

commit v3 on v2

--- a/solution.py
+++ b/solution.py
@@ -17,6 +17,8 @@
 ZSLOT = {z: k for k, z in enumerate(ZREL)}
 ZSLOT[-4] = ZSLOT[4]
 STEP = 256
+EARLY = 6
+PART = 512
 TURNED = 144
 
 NT = (((1,), (1,)), ((), ()))
@@ -52,10 +54,10 @@
 
 def kernel(
     embed_hbm, solution_hbm, targets_hbm, lengths_hbm, ids_hbm, epoch_hbm,
-    row_out, col_out,
+    out,
     embed_ref, solution_ref, targets_ref, lengths_ref, ids_ref, epoch_ref,
     colb, cola, colt, rowe, rowa, rowt, kst, facc, fitb, fit_x, fit_s, fit_y,
-    adjb, acr, idb, perm, dnt, gtb, cgf, cgx, cgr, cgs, cgd, rgb, rgf, rgs, rg_x, rg_s, rg_y,
+    adjb, acr, wgt, idb, perm, dnt, gtb, cgf, cgx, cgr, cgs, cgd, rgb, rgf, rgs, rg_x, rg_s, rg_y,
     ssem, rsem, lsem,
 ):
     h, z, c, x, l = place()
@@ -136,70 +138,88 @@
 
     def gather_rows(ref):
         along_l = [send(ref(0), ref(d), plane_peer(0, -d)) for d in (1, 2, 3)]
-        along_x = [send(ref(0), ref(d * 4), plane_peer(-d, 0)) for d in (2, 1, 3)]
+        along_x = {}
+
+        def go(e, d):
+            along_x[e, d] = send(ref(d), ref(e * 4 + d), plane_peer(-e, 0))
+
+        for e in (1, 3, 2):
+            go(e, 0)
 
         def spread():
             for d, copy in zip((1, 2, 3), along_l):
                 copy.wait_recv()
-                along_x.extend(send(ref(d), ref(e * 4 + d), plane_peer(-e, 0)) for e in (2, 1, 3))
-
-        def finish():
-            for copy in along_x:
-                copy.wait_recv()
+                go(1, d), go(3, d)
+            for d in (1, 2, 3):
+                go(2, d)
+
+        def finish(e):
+            for d in range(4):
+                along_x[e, d].wait_recv()
 
         return spread, finish
 
     spread_rows, finish_rows = gather_rows(lambda s: rowe.at[block(s), :])
 
     arrive(0, -1), arrive(0, 1)
-    arrive(0, -2)
-    forward(0, -2, (2, 1))
-    arrive(0, 2)
-    forward(0, 2, (-1,))
+    spread_rows()
     far_copy.wait_recv()
     forward(1, 0, (-2, 2, -1, 1))
     share(1, 0)
-    spread_rows()
-    arrive(0, -3), arrive(0, 3), arrive(0, 4)
+    arrive(0, 2), arrive(0, -2)
+    forward(0, -2, (2, 1))
+    forward(0, 2, (-1,))
+    for e in (1, 2, 3):
+        finish_rows(e)
+    id_copies = [send(idb.at[0], idb.at[s], plane_peer(-(s // 4), -(s % 4))) for s in range(1, 16)]
+    rowe_all = rowe[...]
+    rowa[:, 0:D] = (rowe_all.astype(F32) * (1.0 / 64)).astype(BF16)
+    rowa[:, D:] = extended(rowe_all, True)
+
+    def columns_in(part):
+        for k in range(4 * part, 4 * part + 4):
+            came[k // 8, k % 8, "core"].wait_recv()
+        cols = slice(part * PART, (part + 1) * PART)
+        embed = colb[cols, 0:D]
+        cola[cols, 0:D] = embed
+        cola[cols, D:] = extended(embed, False)
+
+    def kernel_rows(part, r):
+        rows = slice(r * STEP, (r + 1) * STEP)
+        cols = slice(part * PART, (part + 1) * PART)
+        kern = jnp.exp(lax.dot_general(rowa[rows, :], cola[cols, :], NT, preferred_element_type=F32))
+        kst[2 * part, rows, :] = kern[:, 0:STEP]
+        kst[2 * part + 1, rows, :] = kern[:, STEP:PART]
+
+    def fit_rows(part, r):
+        rows = slice(r * STEP, (r + 1) * STEP)
+        total = None if part == 0 else facc[rows, :]
+        for i in (2 * part, 2 * part + 1):
+            field = colb[i * STEP : (i + 1) * STEP, D : D + E]
+            one = jnp.dot(kst[i, rows, :].astype(BF16), field, preferred_element_type=F32)
+            total = one if total is None else total + one
+        facc[rows, :] = total
+
+    def fit_part(part, done=lambda r: None):
+        columns_in(part)
+        order = (2, 1, 3, 0)
+        kernel_rows(part, order[0])
+        for n, r in enumerate(order):
+            if n < 3:
+                kernel_rows(part, order[n + 1])
+            fit_rows(part, r)
+            done(r)
+
+    fit_part(0)
     arrive(1, 2)
     forward(1, 2, (-2, -1))
     arrive(1, -2)
     forward(1, -2, (1,))
     arrive(1, -1), arrive(1, 1)
-
-    finish_rows()
-    id_copies = [send(idb.at[0], idb.at[s], plane_peer(-(s // 4), -(s % 4))) for s in range(1, 16)]
-    rowe_all = rowe[...]
-    rowa[:, 0:D] = (rowe_all.astype(F32) * (1.0 / 64)).astype(BF16)
-    rowa[:, D:] = extended(rowe_all, True)
-
-    def columns_in(far):
-        for k in range(8):
-            came[far, k, "core"].wait_recv()
-        cols = slice(far * COLS // 2, (far + 1) * COLS // 2)
-        embed = colb[cols, 0:D]
-        cola[cols, 0:D] = embed
-        cola[cols, D:] = extended(embed, False)
-
-    def fit_rows(far, rows, total):
-        for i in range(far * 4, far * 4 + 4):
-            cols = slice(i * STEP, (i + 1) * STEP)
-            power = lax.dot_general(rowa[rows, :], cola[cols, :], NT, preferred_element_type=F32)
-            kern = jnp.exp(power)
-            kst[i, rows, :] = kern
-            part = jnp.dot(kern.astype(BF16), colb[cols, D : D + E], preferred_element_type=F32)
-            total = part if total is None else total + part
-        return total
-
-    columns_in(0)
-
-    @pl.loop(0, ROWS // STEP)
-    def _(r):
-        rows = pl.ds(r * STEP, STEP)
-        facc[rows, :] = fit_rows(0, rows, None)
-
+    arrive(0, -3), arrive(0, 3), arrive(0, 4)
+    fit_part(2)
+    fit_part(1)
     arrive(1, -3), arrive(1, 3), arrive(1, 4)
-    columns_in(1)
 
     def scatter(d, ref, got):
         return {r: send(ref.at[block(4 * d + r), :], got.at[4 * (d - 1) + r], plane_peer(d, 0)) for r in (2, 1, 3, 0)}
@@ -216,21 +236,46 @@
                 last.append(send(going.at[r - 1], ends.at[r - 1], plane_peer(0, r)))
         return last
 
-    fit_copies = {}
-    for d in (2, 1, 3, 0):
-        rows = slice(d * STEP, (d + 1) * STEP)
-        total = fit_rows(1, rows, facc[rows, :])
-        if d:
-            fitb[rows, :] = total.astype(BF16)
-            fit_copies[d] = scatter(d, fitb, fit_x)
+    passing, below, above = {}, {}, {}
+
+    def put(d, r, slot, step):
+        return send(fitb.at[block(4 * d + r), :], fit_x.at[slot], plane_peer(step, 0))
+
+    def leave(d):
+        if d == 2:
+            rows = slice(d * STEP, (d + 1) * STEP)
+            fitb[rows, :] = facc[rows, :].astype(BF16)
+            for r in (2, 3, 1, 0):
+                passing[r] = put(2, r, 8 + r, 1 if r in (1, 2) else -1)
+        if d == 1:
+            for r in (3, 0):
+                fitb[block(4 + r), :] = facc[block(4 + r), :].astype(BF16)
+                below[r] = put(1, r, r, 1)
+        if d == 3:
+            for r in (2, 1):
+                fitb[block(12 + r), :] = facc[block(12 + r), :].astype(BF16)
+                above[r] = put(3, r, 4 + r, -1)
+
+    fit_part(3, leave)
+    for r in (2, 3, 1, 0):
+        passing[r].wait_recv()
+        d = 1 if r in (1, 2) else 3
+        fitb[block(4 * d + r), :] = (facc[block(4 * d + r), :] + fit_x[8 + r].astype(F32)).astype(BF16)
+        if d == 1:
+            below[r] = put(1, r, r, 1)
         else:
-            facc[rows, :] = total
-
-    fit_last = reduce_rows(fit_copies, facc, fit_x, fit_s, fit_y)
+            above[r] = put(3, r, 4 + r, -1)
+    fit_last = []
+    for r in (2, 3, 1, 0):
+        below[r].wait_recv()
+        above[r].wait_recv()
+        facc[block(r), :] += fit_x[r].astype(F32) + fit_x[4 + r].astype(F32)
+        if r:
+            fit_s[r - 1] = facc[block(r), :].astype(BF16)
+            fit_last.append(send(fit_s.at[r - 1], fit_y.at[r - 1], plane_peer(0, r)))
 
     rowt[...] = rowa[...].T[0:TURNED]
     colt[...] = colb[:, 0:D].T
-    acr[...] = jnp.zeros_like(acr)
     for copy in id_copies:
         copy.wait_recv()
     lane = lax.broadcasted_iota(I32, (1, 128), 1)
@@ -252,7 +297,7 @@
     epoch = lax.broadcasted_iota(I32, (OWN, E), 1).astype(F32)
 
     total = facc[0:OWN, :]
-    for r, copy in enumerate(fit_last):
+    for copy in fit_last:
         copy.wait_recv()
     total += sum(fit_y[r].astype(F32) for r in range(3))
     adjoint = jnp.where(epoch < span, targets_ref[...].astype(F32) - total, 0.0).astype(BF16)
@@ -260,19 +305,55 @@
     spread_adjoint, finish_adjoint = gather_rows(lambda s: adjb.at[block(s), :])
     spread_adjoint()
 
-    def grad_rows(i, rows):
-        cols = pl.ds(i * STEP, STEP)
+    def weigh(i, rows):
+        cols = slice(i * STEP, (i + 1) * STEP)
         link = lax.dot_general(adjb[rows, :], colb[cols, D : D + E], NT, preferred_element_type=F32)
-        weight = (link * kst[i, rows, :]).astype(BF16)
-        acr[rows, :] += jnp.dot(weight, cola[cols, :], preferred_element_type=F32)
-        return jnp.dot(rowt[:, rows], weight, preferred_element_type=F32)
-
-    @pl.loop(0, COLS // STEP, step=2)
-    def _(i):
-        for j in (i, i + 1):
-            dnt[j] = grad_rows(j, slice(0, STEP))
-
-    finish_adjoint()
+        wgt[i, rows, :] = (link * kst[i, rows, :]).astype(BF16)
+
+    def across(i, rows):
+        part = jnp.dot(wgt[i, rows, :], cola[i * STEP : (i + 1) * STEP, :], preferred_element_type=F32)
+        if i == order[0]:
+            acr[rows, :] = part
+        else:
+            acr[rows, :] += part
+
+    def down(i, rows):
+        return jnp.dot(rowt[:, rows], wgt[i, rows, :], preferred_element_type=F32)
+
+    order = (7, 6, 5, 4, 3, 2, 1, 0)
+
+    def rows_arrived(e):
+        rows = slice(e * STEP, (e + 1) * STEP)
+        weigh(order[0], rows)
+        for n, i in enumerate(order):
+            if n < 7:
+                weigh(order[n + 1], rows)
+            across(i, rows)
+            part = down(i, rows)
+            if e == 0:
+                dnt[i] = part
+            else:
+                dnt[i] += part
+
+    rows_arrived(0)
+    finish_adjoint(1)
+    rows_arrived(1)
+    finish_adjoint(3)
+    finish_adjoint(2)
+
+    def finish(i, n):
+        total = dnt[i] + down(i, rest)
+        gtb[n] = total[0:D] * 64.0 - colt[:, i * STEP : (i + 1) * STEP].astype(F32) * total[D : D + 1]
+
+    def turn(i, n):
+        turned = gtb[n].T
+        for s in range(2):
+            cgf[2 * i + s] = turned[2 * s * OWN : (2 * s + 1) * OWN]
+            cgx[2 * i + s] = turned[(2 * s + 1) * OWN : (2 * s + 2) * OWN].astype(BF16)
+
+    def swap(i):
+        pair = pl.ds(2 * i, 2)
+        swaps[i] = send(cgx.at[pair], cgr.at[pair], core_peer)
 
     col_copies = []
     swaps = {}
@@ -287,27 +368,19 @@
             owner = at((h + far) % 2, (z + zrel + 8) % 8, c, x, l)
             col_copies.append((k, send(cgs.at[k], cgd.at[k], owner)))
 
-    def turn(i, n):
-        turned = gtb[n % 2].T
-        for s in range(2):
-            cgf[2 * i + s] = turned[2 * s * OWN : (2 * s + 1) * OWN]
-            cgx[2 * i + s] = turned[(2 * s + 1) * OWN : (2 * s + 2) * OWN].astype(BF16)
-
-    def swap(i):
-        pair = pl.ds(2 * i, 2)
-        swaps[i] = send(cgx.at[pair], cgr.at[pair], core_peer)
-
-    order = (7, 6, 5, 3, 4, 2, 1, 0)
+    rest = slice(2 * STEP, ROWS)
+    weigh(order[0], rest)
     for n, i in enumerate(order):
-        down = dnt[i] + grad_rows(i, slice(STEP, ROWS))
-        gtb[n % 2] = down[0:D] * 64.0 - colt[:, i * STEP : (i + 1) * STEP].astype(F32) * down[D : D + 1]
-        if n:
+        if n < 7:
+            weigh(order[n + 1], rest)
+        across(i, rest)
+        if n < EARLY:
+            finish(i, n)
+        if 0 < n <= EARLY:
             turn(order[n - 1], n - 1)
             swap(order[n - 1])
-        if n > 1:
-            add_cores(order[n - 2])
-    turn(0, 7)
-    swap(0)
+        if n > 3:
+            add_cores(order[n - 4])
 
     sums = acr[:, D + 3 : D + 4]
     rgb[...] = (acr[:, 0:D] - rowe[...].astype(F32) * sums).astype(BF16)
@@ -323,21 +396,27 @@
         rgs[d * STEP : (d + 1) * STEP, :] = placed(d).astype(BF16)
         row_copies[d] = scatter(d, rgs, rg_x)
     rgf[...] = placed(0)
-    add_cores(order[-2])
-    add_cores(order[-1])
+    for n in range(4, EARLY):
+        add_cores(order[n])
+    for n in range(EARLY, 8):
+        finish(order[n], n)
+        turn(order[n], n)
+        swap(order[n])
+    for n in range(EARLY, 8):
+        add_cores(order[n])
 
     row_last = reduce_rows(row_copies, rgf, rg_x, rg_s, rg_y)
     for copy in row_last:
         copy.wait_recv()
     row_total = rgf[0:OWN, :] + sum(rg_y[r].astype(F32) for r in range(3))
-    row_out[...] = row_total * (2.0 / D)
+    out[0] = row_total * (2.0 / D)
 
     for k, copy in col_copies:
         copy.wait_recv()
     col_total = cgf[0] + cgr[0].astype(F32)
     for k, copy in col_copies:
         col_total += cgd[k].astype(F32)
-    col_out[...] = col_total * (2.0 / D)
+    out[1] = col_total * (2.0 / D)
     for copy in sent:
         copy.wait_send()
 
@@ -349,17 +428,17 @@
         ((COLS, D + E), BF16), ((COLS, 2 * D), BF16), ((D, COLS), BF16), ((ROWS, D), BF16), ((ROWS, 2 * D), BF16),
         ((TURNED, ROWS), BF16), ((COLS // STEP, ROWS, STEP), F32), ((ROWS, E), F32), ((ROWS, E), BF16),
         ((12, OWN, E), BF16), ((3, OWN, E), BF16), ((3, OWN, E), BF16),
-        ((ROWS, E), BF16), ((ROWS, 2 * D), F32), ((16, 8, 128), I32), ((4, ROWS, STEP), BF16),
-        ((COLS // STEP, TURNED, STEP), F32), ((2, D, STEP), F32),
+        ((ROWS, E), BF16), ((ROWS, 2 * D), F32), ((COLS // STEP, ROWS, STEP), BF16), ((16, 8, 128), I32), ((4, ROWS, STEP), BF16),
+        ((COLS // STEP, TURNED, STEP), F32), ((8, D, STEP), F32),
         ((16, OWN, D), F32), ((16, OWN, D), BF16), ((16, OWN, D), BF16), ((16, OWN, D), BF16),
         ((16, OWN, D), BF16), ((ROWS, D), BF16), ((STEP, D), F32), ((ROWS, D), BF16),
         ((12, OWN, D), BF16), ((3, OWN, D), BF16), ((3, OWN, D), BF16),
     ]
-    return pl.pallas_call(
+    both = pl.pallas_call(
         kernel,
-        out_shape=(jax.ShapeDtypeStruct((OWN, D), F32), jax.ShapeDtypeStruct((OWN, D), F32)),
+        out_shape=jax.ShapeDtypeStruct((2, OWN, D), F32),
         in_specs=[pl.BlockSpec(memory_space=pl.ANY)] * 6,
-        out_specs=(vmem, vmem),
+        out_specs=vmem,
         scratch_shapes=[pltpu.VMEM(s, t) for s, t in scratch]
         + [pltpu.SemaphoreType.DMA((160,)), pltpu.SemaphoreType.DMA((160,)), pltpu.SemaphoreType.DMA((6,))],
         compiler_params=pltpu.CompilerParams(
@@ -367,6 +446,7 @@
         ),
         name="tile",
     )(curve_embed, solution, targets, lengths.reshape(1, OWN), slot_curve.reshape(1, OWN), epoch_kernel)
+    return both[0], both[1]
 
 
 def solution(mesh):

time: 74.3 us -> 71.5 us (0.962)
  Pallas kernels: 71.4 us -> 69.2 us
    pallas_call x1, Pallas kernels: 71.4 us -> 69.2 us  [per_device(): pl.pallas_call(kernel, out_shape=jax.ShapeDtypeStruct((2, OWN, D), F32),...]
    unnamed x4 -> x0, local copies, waits for them, and re-layouts: 2 us -> none
    squeeze x0 -> x1, local copies, waits for them, and re-layouts: none -> 1.4 us  [per_device(): return (both[0], both[1])]
where the time goes in v3:
time: 71.5 us; the launch traced here: 71.3 us
  Pallas kernels  69.2 us (97%)
  local copies, waits for them, and re-layouts  1.4 us (2%)
    pallas_call x1, Pallas kernels, per_device(): pl.pallas_call(kernel, out_shape=jax.ShapeDtypeStruct((2, OWN, D), F32),...  69.2 us

profile of v3, /device:TPU:1, one launch (start us, length us, event | category | flops | bytes accessed | tf_op | source)
XLA Modules:
  0.0 71.3 jit_solution(103784371217867256)
XLA Ops:
  0.6 69.2 %tile.1 = f32[2,64,128]{2,1,0:T(8,128)} custom-call(bf16[64,128]{1,0:T(8,128)(2,1)} %embed_hbm.1, f32[64,256]{1,0:T(8,128)} %solution_hbm.1, bf16[64,256]{1,0:T(8,128)(2,1)} %targets_hbm.1, s32[1,64]{1,0:T(1,128)} %bitcast.6, s32[1,64]{1,0:T(1,128)} %bitcast.7, f32[256,256]{1,0:T(8,128)} %epoch_hbm.1), custom_call_target="tpu_custom_call" | custom-call | tf_op jit(solution)/shard_map/tile/pallas_call | solution.py:437
  69.9 1.4 %slice_bitcast_fusion = (f32[64,128]{1,0:T(8,128)}, f32[64,128]{1,0:T(8,128)}) fusion(f32[2,64,128]{2,1,0:T(8,128)} %tile.1), kind=kLoop, calls=%fused_computation | loop fusion | bytes 131072 | tf_op jit(solution)/shard_map/squeeze | solution.py:449

commit v4 on v3

--- a/solution.py
+++ b/solution.py
@@ -76,7 +76,7 @@
         return copy
 
     core_peer = at(h, z, 1 - c, x, l)
-    far_peer = at(1 - h, z, c, x, l)
+    far_peer = at(1 - h, z, c, x, 3 - l)
     z_peer = lambda d: at(h, (z + d + 8) % 8, c, x, l)
     plane_peer = lambda dx, dl: at(h, z, c, (x + dx + 4) % 4, (l + dl + 4) % 4)
 
@@ -163,12 +163,13 @@
 
     arrive(0, -1), arrive(0, 1)
     spread_rows()
+    arrive(0, -2)
+    forward(0, -2, (2, 1))
+    arrive(0, 2)
+    forward(0, 2, (-1,))
     far_copy.wait_recv()
     forward(1, 0, (-2, 2, -1, 1))
     share(1, 0)
-    arrive(0, 2), arrive(0, -2)
-    forward(0, -2, (2, 1))
-    forward(0, 2, (-1,))
     for e in (1, 2, 3):
         finish_rows(e)
     id_copies = [send(idb.at[0], idb.at[s], plane_peer(-(s // 4), -(s % 4))) for s in range(1, 16)]
@@ -365,7 +366,7 @@
                 continue
             far, zrel = k // 8, ZREL[k % 8]
             cgs[k] = (cgf[k] + cgr[k].astype(F32)).astype(BF16)
-            owner = at((h + far) % 2, (z + zrel + 8) % 8, c, x, l)
+            owner = at((h + far) % 2, (z + zrel + 8) % 8, c, x, 3 - l if far else l)
             col_copies.append((k, send(cgs.at[k], cgd.at[k], owner)))
 
     rest = slice(2 * STEP, ROWS)
@@ -379,9 +380,9 @@
         if 0 < n <= EARLY:
             turn(order[n - 1], n - 1)
             swap(order[n - 1])
-        if n > 3:
-            add_cores(order[n - 4])
-
+
+    for i in order[:4]:
+        add_cores(i)
     sums = acr[:, D + 3 : D + 4]
     rgb[...] = (acr[:, 0:D] - rowe[...].astype(F32) * sums).astype(BF16)
 

time: 71.5 us -> 69.8 us (0.976)
  Pallas kernels: 69.2 us -> 67.5 us
    pallas_call x1, Pallas kernels: 69.2 us -> 67.5 us  [per_device(): pl.pallas_call(kernel, out_shape=jax.ShapeDtypeStruct((2, OWN, D), F32),...]
where the time goes in v4:
time: 69.8 us; the launch traced here: 69.6 us
  Pallas kernels  67.5 us (97%)
  local copies, waits for them, and re-layouts  1.4 us (2%)
    pallas_call x1, Pallas kernels, per_device(): pl.pallas_call(kernel, out_shape=jax.ShapeDtypeStruct((2, OWN, D), F32),...  67.5 us
    squeeze x1, local copies, waits for them, and re-layouts, per_device(): return (both[0], both[1])  1.4 us

profile of v4, /device:TPU:1, one launch (start us, length us, event | category | flops | bytes accessed | tf_op | source)
XLA Modules:
  0.0 69.6 jit_solution(9581952282617978951)
XLA Ops:
  0.6 67.5 %tile.1 = f32[2,64,128]{2,1,0:T(8,128)} custom-call(bf16[64,128]{1,0:T(8,128)(2,1)} %embed_hbm.1, f32[64,256]{1,0:T(8,128)} %solution_hbm.1, bf16[64,256]{1,0:T(8,128)(2,1)} %targets_hbm.1, s32[1,64]{1,0:T(1,128)} %bitcast.6, s32[1,64]{1,0:T(1,128)} %bitcast.7, f32[256,256]{1,0:T(8,128)} %epoch_hbm.1), custom_call_target="tpu_custom_call" | custom-call | tf_op jit(solution)/shard_map/tile/pallas_call | solution.py:438
  68.2 1.4 %slice_bitcast_fusion = (f32[64,128]{1,0:T(8,128)}, f32[64,128]{1,0:T(8,128)}) fusion(f32[2,64,128]{2,1,0:T(8,128)} %tile.1), kind=kLoop, calls=%fused_computation | loop fusion | bytes 131072 | tf_op jit(solution)/shard_map/squeeze | solution.py:450

commit v5 on v4

--- a/solution.py
+++ b/solution.py
@@ -381,8 +381,6 @@
             turn(order[n - 1], n - 1)
             swap(order[n - 1])
 
-    for i in order[:4]:
-        add_cores(i)
     sums = acr[:, D + 3 : D + 4]
     rgb[...] = (acr[:, 0:D] - rowe[...].astype(F32) * sums).astype(BF16)
 
@@ -397,7 +395,7 @@
         rgs[d * STEP : (d + 1) * STEP, :] = placed(d).astype(BF16)
         row_copies[d] = scatter(d, rgs, rg_x)
     rgf[...] = placed(0)
-    for n in range(4, EARLY):
+    for n in range(EARLY):
         add_cores(order[n])
     for n in range(EARLY, 8):
         finish(order[n], n)

time: 69.8 us -> 68.9 us (0.987)
  Pallas kernels: 67.5 us -> 66 us
    pallas_call x1, Pallas kernels: 67.5 us -> 66 us  [per_device(): pl.pallas_call(kernel, out_shape=jax.ShapeDtypeStruct((2, OWN, D), F32),...]
where the time goes in v5:
time: 68.9 us; the launch traced here: 68 us
  Pallas kernels  66 us (96%)
  local copies, waits for them, and re-layouts  1.4 us (2%)
    pallas_call x1, Pallas kernels, per_device(): pl.pallas_call(kernel, out_shape=jax.ShapeDtypeStruct((2, OWN, D), F32),...  66 us
    squeeze x1, local copies, waits for them, and re-layouts, per_device(): return (both[0], both[1])  1.4 us

profile of v5, /device:TPU:1, one launch (start us, length us, event | category | flops | bytes accessed | tf_op | source)
XLA Modules:
  0.0 68.0 jit_solution(3405579334919999968)
XLA Ops:
  0.6 66.0 %tile.1 = f32[2,64,128]{2,1,0:T(8,128)} custom-call(bf16[64,128]{1,0:T(8,128)(2,1)} %embed_hbm.1, f32[64,256]{1,0:T(8,128)} %solution_hbm.1, bf16[64,256]{1,0:T(8,128)(2,1)} %targets_hbm.1, s32[1,64]{1,0:T(1,128)} %bitcast.6, s32[1,64]{1,0:T(1,128)} %bitcast.7, f32[256,256]{1,0:T(8,128)} %epoch_hbm.1), custom_call_target="tpu_custom_call" | custom-call | tf_op jit(solution)/shard_map/tile/pallas_call | solution.py:436
  66.6 1.4 %slice_bitcast_fusion = (f32[64,128]{1,0:T(8,128)}, f32[64,128]{1,0:T(8,128)}) fusion(f32[2,64,128]{2,1,0:T(8,128)} %tile.1), kind=kLoop, calls=%fused_computation | loop fusion | bytes 131072 | tf_op jit(solution)/shard_map/squeeze | solution.py:448

commit v6 on v5

--- a/solution.py
+++ b/solution.py
@@ -17,7 +17,7 @@
 ZSLOT = {z: k for k, z in enumerate(ZREL)}
 ZSLOT[-4] = ZSLOT[4]
 STEP = 256
-EARLY = 6
+EARLY = 4
 PART = 512
 TURNED = 144
 

time: 68.9 us -> 70.6 us (1.025)
  Pallas kernels: 66 us -> 68.3 us
    pallas_call x1, Pallas kernels: 66 us -> 68.3 us  [per_device(): pl.pallas_call(kernel, out_shape=jax.ShapeDtypeStruct((2, OWN, D), F32),...]
where the time goes in v6:
time: 70.6 us; the launch traced here: 70.4 us
  Pallas kernels  68.3 us (97%)
  local copies, waits for them, and re-layouts  1.4 us (2%)
    pallas_call x1, Pallas kernels, per_device(): pl.pallas_call(kernel, out_shape=jax.ShapeDtypeStruct((2, OWN, D), F32),...  68.3 us

profile of v6, /device:TPU:1, one launch (start us, length us, event | category | flops | bytes accessed | tf_op | source)
XLA Modules:
  0.0 70.4 jit_solution(8153245541375178210)
XLA Ops:
  0.6 68.3 %tile.1 = f32[2,64,128]{2,1,0:T(8,128)} custom-call(bf16[64,128]{1,0:T(8,128)(2,1)} %embed_hbm.1, f32[64,256]{1,0:T(8,128)} %solution_hbm.1, bf16[64,256]{1,0:T(8,128)(2,1)} %targets_hbm.1, s32[1,64]{1,0:T(1,128)} %bitcast.6, s32[1,64]{1,0:T(1,128)} %bitcast.7, f32[256,256]{1,0:T(8,128)} %epoch_hbm.1), custom_call_target="tpu_custom_call" | custom-call | tf_op jit(solution)/shard_map/tile/pallas_call | solution.py:436
  69.0 1.4 %slice_bitcast_fusion = (f32[64,128]{1,0:T(8,128)}, f32[64,128]{1,0:T(8,128)}) fusion(f32[2,64,128]{2,1,0:T(8,128)} %tile.1), kind=kLoop, calls=%fused_computation | loop fusion | bytes 131072 | tf_op jit(solution)/shard_map/squeeze | solution.py:448
